TPU v7x, 128 devices: a whole 4x4x4 slice. The times are simulated.
128 devices in a mesh: half: 2 (over y_hi), row: 8 (over y_lo, z), col: 8 (over x, core).
Axes of the slice: x: 4, y: 4 (y_hi: 2, y_lo: 2; y = y_hi * 2 + y_lo), z: 4, core: 2. Of those that a mesh axis runs over, the one named last changes fastest.
Arguments:
- child_block: bfloat16 [2, 8, 8, 256, 8, 8, 256], P('half', None, 'row', None, None, 'col'), may hold values from -6 to 6
- child_row: bfloat16 [2, 256, 8, 8, 256], P('half', 'row', None, 'col'), may hold values from -6 to 6
- child_col: bfloat16 [2, 256, 8, 8, 256], P('half', 'col', None, 'row'), may hold values from -0.375 to 0.375
- child_pivot_inv: bfloat16 [2, 256, 256], P('half'), may hold values from -0.375 to 0.375
- child_map: int32 [2, 64], replicated, may hold values from 0 to 126, as said below
- parent_row: bfloat16 [256, 8, 16, 256], P('row', None, ('half', 'col')), may hold values from -6 to 6
- parent_col: bfloat16 [256, 16, 8, 256], P(('half', 'col'), None, 'row'), may hold values from -0.375 to 0.375
- parent_pivot_inv: bfloat16 [256, 256], replicated, may hold values from -0.375 to 0.375
- parent_diag: float32 [16, 8, 256], P(None, 'row'), may hold values from 1 to 3
Outputs:
- schur: bfloat16 [16, 8, 256, 8, 16, 256], P(None, 'row', None, None, ('half', 'col'))
Inputs may be any that keep to these rules, and one draw needn't show every extreme that they name: child_map[h, 8 * k + r] = 2 * 8 * k + r + p_h[k] for k and r from 0 to 7, where p_0 and p_1 are permutations of 0 to 7.
All inputs are finite; a program needn't handle non-finite values.
Results may differ from a plain program's by a relative error of at most 0.0041.
The roundings to bfloat16 on the way count: a program that leaves them out, or rounds other values in their place, can miss the bound.
Values may be sent and summed in bfloat16 or wider, within the bound.
A program may use at most 384 MiB of HBM per device.

v0:
```python
import jax
import jax.numpy as jnp
from jax import lax
from jax.sharding import PartitionSpec as P


def inverse_maps(child_map, parent_tiles):
    targets = jnp.arange(parent_tiles, dtype=jnp.int32)
    matches = child_map[:, None, :] == targets[None, :, None]
    covered = jnp.any(matches, axis=2)
    positions = jnp.arange(child_map.shape[1], dtype=jnp.int32)
    sources = jnp.sum(jnp.where(matches, positions[None, None, :], 0), axis=2)
    return (covered, sources)


def pick_index(keys, wanted):
    positions = jnp.arange(keys.shape[0], dtype=jnp.int32)
    matched = keys[None, :] == wanted[:, None]
    return (jnp.sum(jnp.where(matched, positions[None, :], 0), axis=1), jnp.any(matched, axis=1))


def shards(
    child_block,
    child_row,
    child_col,
    child_pivot_inv,
    child_map,
    parent_row,
    parent_col,
    parent_pivot_inv,
    parent_diag,
):
    grid_size = lax.axis_size("row")
    tile_width = child_pivot_inv.shape[-1]
    my_half = lax.axis_index("half")
    my_row = lax.axis_index("row")
    my_col = lax.axis_index("col")
    local_width = grid_size * tile_width
    parent_height = 2 * grid_size * tile_width
    child_inv = child_pivot_inv[0]
    pieces = (
        lax.all_gather(child_row[0], "row", axis=0, tiled=True),
        lax.all_gather(parent_row, "row", axis=0, tiled=True),
    )
    piece_rows = pieces[0].shape[0]
    child_piece = pieces[0].reshape(piece_rows, local_width)
    parent_piece = pieces[1].reshape(piece_rows, local_width)
    child_sum = jnp.dot(child_inv, child_piece, preferred_element_type=jnp.float32)
    parent_sum = jnp.dot(parent_pivot_inv, parent_piece, preferred_element_type=jnp.float32)
    child_scaled = child_sum
    parent_scaled = parent_sum
    child_scaled = child_scaled.astype(jnp.bfloat16)
    parent_scaled = parent_scaled.astype(jnp.bfloat16)
    piece = lax.all_gather(child_col, "col", axis=1, tiled=True)
    piece_rows = piece.shape[1]
    flattened = piece.reshape(piece_rows, local_width)
    scaled_part = child_scaled
    child_update = lax.dot_general(
        flattened, scaled_part, (((0,), (0,)), ((), ())), preferred_element_type=jnp.float32
    )
    contribution = (
        child_block.reshape(local_width, local_width).astype(jnp.float32) - child_update
    ).astype(jnp.bfloat16)
    tile_grid = contribution.reshape(grid_size, tile_width, grid_size, tile_width)
    parent_rows = grid_size * jnp.arange(2 * grid_size, dtype=jnp.int32) + my_row
    column_slot = my_half * grid_size + my_col
    parent_columns = 2 * grid_size * jnp.arange(grid_size, dtype=jnp.int32) + column_slot
    diag_values = parent_diag.reshape(2 * grid_size, tile_width)
    on_diagonal = (parent_rows[:, None] == parent_columns[None, :]).astype(jnp.float32)
    identity = jnp.eye(tile_width, dtype=jnp.float32)
    diag_term = (
        diag_values[:, :, None, None] * on_diagonal[:, None, :, None] * identity[None, :, None, :]
    ).reshape(parent_height, local_width)
    piece = lax.all_gather(parent_col, ("half", "col"), axis=0, tiled=True)
    piece_rows = piece.shape[0]
    flattened = piece.reshape(piece_rows, parent_height)
    scaled_part = parent_scaled
    parent_front = diag_term - lax.dot_general(
        flattened, scaled_part, (((0,), (0,)), ((), ())), preferred_element_type=jnp.float32
    )
    covered, sources = inverse_maps(child_map, 2 * grid_size * grid_size)
    own_map = jnp.take(child_map, my_half, axis=0).reshape(grid_size, grid_size)
    row_targets = lax.dynamic_index_in_dim(own_map, my_row, 1, keepdims=False)
    col_targets = lax.dynamic_index_in_dim(own_map, my_col, 1, keepdims=False)
    slots_small = jnp.arange(grid_size, dtype=jnp.int32)
    row_pick, row_found = pick_index(row_targets % grid_size, slots_small)
    row_covered = covered[:, parent_rows]
    row_source = sources[:, parent_rows] % grid_size
    col_covered = covered[:, parent_columns]
    col_source = sources[:, parent_columns] % grid_size
    usable = row_covered[:, :, None] & col_covered[:, None, :]
    by_rows = jnp.take(tile_grid, row_pick, axis=0)
    column_slots = jnp.arange(2 * grid_size, dtype=jnp.int32)
    col_pick, col_live = pick_index(col_targets % (2 * grid_size), column_slots)
    packed = jnp.take(by_rows, col_pick, axis=2)
    packed = jnp.where(col_live[None, None, :, None], packed, jnp.zeros((), jnp.bfloat16))
    moved_rows = lax.all_to_all(packed, "row", split_axis=0, concat_axis=0, tiled=True)
    arrived = lax.all_to_all(moved_rows, ("half", "col"), split_axis=2, concat_axis=2, tiled=True)
    sibling_pieces = []
    for sibling in range(2):
        picked = jnp.take(arrived, row_source[sibling], axis=0)
        sibling_pieces.append(jnp.take(picked, sibling * grid_size + col_source[sibling], axis=2))
    front_blocks = parent_front.reshape(2 * grid_size, tile_width, grid_size, tile_width)
    for sibling in range(2):
        mask = usable[sibling][:, None, :, None]
        front_blocks = front_blocks + jnp.where(
            mask, sibling_pieces[sibling].astype(jnp.float32), 0.0
        )
    schur_front = front_blocks.astype(jnp.bfloat16)
    return schur_front.reshape(2 * grid_size, 1, tile_width, grid_size, 1, tile_width)


def solution(mesh):
    return jax.shard_map(
        shards,
        mesh=mesh,
        in_specs=(
            P("half", None, "row", None, None, "col", None),
            P("half", "row", None, "col", None),
            P("half", "col", None, "row", None),
            P("half", None, None),
            P(),
            P("row", None, ("half", "col"), None),
            P(("half", "col"), None, "row", None),
            P(),
            P(None, "row", None),
        ),
        out_specs=P(None, "row", None, None, ("half", "col"), None),
        check_vma=False,
    )
```

profile of v0, /device:TPU:1, one launch (start us, length us, event | category | flops | bytes accessed | tf_op | source)
XLA Modules:
  0.0 912.3 jit_solution(1902297807044894404)
XLA Ops:
  8.8 13.8 %copy.75 = f32[256,8,8,256]{3,1,2,0:T(8,128)} copy(bf16[256,8,8,256]{3,2,1,0:T(8,128)(2,1)} %bitcast.101) | data formatting | bytes 25165824
  22.6 18.1 %copy.67 = f32[2048,2048]{0,1:T(8,128)} copy(f32[2048,2048]{1,0:T(8,128)} %bitcast.94) | data formatting | bytes 33554432 | tf_op jit(solution)/shard_map/convert_element_type | solution.py:62
  47.6 28.0 %all-gather.10.cloned.1.call-done = bf16[1,256,8,1,256]{4,2,3,0,1:T(8,128)(2,1)} async-done(((bf16[1,32,8,1,256]{4,2,3,0,1:T(8,128)(2,1)}), bf16[1,256,8,1,256]{4,2,3,0,1:T(8,128)(2,1)}) %all-gather.10.cloned.1.call-update) | async-done | bytes 1048592 | tf_op jit(solution)/shard_map/all_gather | solution.py:54
  77.1 9.3 %fusion.1 = bf16[2048,2048]{0,1:T(8,128)(2,1)} fusion(f32[2048,2048]{0,1:T(8,128)} %copy.67, bf16[256,2048]{1,0:T(8,128)(2,1)S(1)} %bitcast.105, bf16[256,2048]{1,0:T(8,128)(2,1)S(1)} %bitcast.104, bf16[1,256,256]{2,1,0:T(8,128)(2,1)S(1)} %copy-done.2), kind=kOutput, calls=%fused_computation.22 | convolution fusion | flops 2424832000 | bytes 27394048 | tf_op jit(solution)/shard_map/dot_general | solution.py:58
  86.4 10.3 %copy.78 = bf16[256,8,8,256]{3,2,1,0:T(8,128)(2,1)} copy(bf16[256,8,8,256]{3,1,2,0:T(8,128)(2,1)} %bitcast.99) | data formatting | bytes 16777216
  96.7 12.6 %copy.58 = bf16[8,256,8,256]{3,1,2,0:T(8,128)(2,1)} copy(bf16[8,256,8,256]{1,0,3,2:T(8,128)(2,1)} %bitcast.100) | data formatting | bytes 16777216 | tf_op jit(solution)/shard_map/reshape | solution.py:64
  109.3 8.1 gather_fusion.2
  124.8 10.7 %gather_fusion.3 = bf16[16,8,256,256]{3,2,1,0:T(8,128)(2,1)} fusion(bf16[8,256,8,256]{3,1,2,0:T(8,128)(2,1)} %broadcast_select_fusion, s32[1024]{0:T(1024)S(1)} %pad_clamp_fusion.4), kind=kCustom, calls=%fused_computation.11 | custom fusion | bytes 33554496 | tf_op jit(solution)/shard_map/jit(_take)/gather | solution.py:95
  135.6 8.7 select_bitcast_fusion
  146.5 187.8 %all_to_all.10 = bf16[8,256,16,256]{3,1,2,0:T(8,128)(2,1)S(1)} all-to-all(bf16[8,256,16,256]{3,1,2,0:T(8,128)(2,1)S(1)} %copy.59), channel_id=1, replica_groups=mesh['half'=2,'row'=8,'col'=8] {'row'}, dimensions={0} | all-to-all | bytes 33554432 | tf_op jit(solution)/shard_map/all_to_all | solution.py:97
  357.2 36.2 %copy.71 = f32[256,8,16,256]{3,1,2,0:T(8,128)} copy(f32[256,8,16,256]{3,2,1,0:T(8,128)S(1)} %bitcast.92) | data formatting | bytes 67108864
  396.8 93.5 %all-gather.6.cloned.1.call-done = bf16[256,8,1,256]{3,1,2,0:T(8,128)(2,1)} async-done(((bf16[32,8,1,256]{3,1,2,0:T(8,128)(2,1)}), bf16[256,8,1,256]{3,1,2,0:T(8,128)(2,1)}) %all-gather.6.cloned.1.call-update) | async-done | bytes 1048592 | tf_op jit(solution)/shard_map/all_gather | solution.py:43
  491.9 88.7 %all-gather.8.cloned.1.call-done = bf16[256,16,1,256]{3,1,2,0:T(8,128)(2,1)} async-done(((bf16[16,16,1,256]{3,1,2,0:T(8,128)(2,1)}), bf16[256,16,1,256]{3,1,2,0:T(8,128)(2,1)}) %all-gather.8.cloned.1.call-update) | async-done | bytes 2097168 | tf_op jit(solution)/shard_map/all_gather | solution.py:74
  583.1 21.5 %bitcast_subtract_fusion = f32[4096,2048]{0,1:T(8,128)} fusion(f32[4096,2048]{0,1:T(8,128)} %bitcast.90, bf16[256,4096]{1,0:T(8,128)(2,1)S(1)} %bitcast.102, bf16[256,256]{1,0:T(8,128)(2,1)S(1)} %copy-done, bf16[256,2048]{1,0:T(8,128)(2,1)S(1)} %bitcast.103), kind=kOutput, calls=%fused_computation.16 | convolution fusion | flops 4572315648 | bytes 70385664 | tf_op jit(solution)/shard_map/dot_general | solution.py:78
  604.5 30.2 %copy.74 = f32[256,8,16,256]{3,2,1,0:T(8,128)} copy(f32[256,8,16,256]{3,1,2,0:T(8,128)} %bitcast.91) | data formatting | bytes 67108864
  634.7 34.4 %copy.63 = f32[16,256,8,256]{3,1,0,2:T(8,128)} copy(f32[16,256,8,256]{1,0,3,2:T(8,128)} %bitcast.93) | data formatting | bytes 67108864 | tf_op jit(solution)/shard_map/reshape | solution.py:103
  669.2 12.0 %fusion.18 = (bf16[8,128,16,256]{3,1,0,2:T(8,128)(2,1)}, bf16[8,128,16,256]{3,1,0,2:T(8,128)(2,1)}) fusion(bf16[8,256,16,256]{3,1,0,2:T(8,128)(2,1)} %all-to-all-done.1), kind=kLoop, calls=%fused_computation.102 | loop fusion | bytes 33554432 | tf_op jit(solution)/shard_map/jit(_take)/gather | solution.py:101
  688.9 7.7 copy.70
  696.6 10.5 %gather_fusion.11 = bf16[16,128,16,256]{3,1,2,0:T(8,128)(2,1)} fusion(bf16[8,128,16,256]{3,1,2,0:T(8,128)(2,1)} %copy.70, s32[1024]{0:T(1024)S(1)} %pad_clamp_fusion.1), kind=kCustom, calls=%fused_computation.5.clone | custom fusion | bytes 33554496 | tf_op jit(solution)/shard_map/jit(_take)/gather | solution.py:101
  707.1 10.6 %gather_fusion.7 = bf16[16,128,16,256]{3,1,2,0:T(8,128)(2,1)} fusion(bf16[8,128,16,256]{3,1,2,0:T(8,128)(2,1)} %copy.70, s32[1024]{0:T(1024)S(1)} %pad_clamp_fusion.3), kind=kCustom, calls=%fused_computation.1.clone | custom fusion | bytes 33554496 | tf_op jit(solution)/shard_map/jit(_take)/gather | solution.py:101
  717.7 10.4 %gather_fusion.6 = bf16[16,128,16,256]{3,1,2,0:T(8,128)(2,1)} fusion(bf16[8,128,16,256]{3,1,2,0:T(8,128)(2,1)} %copy.69, s32[1024]{0:T(1024)S(1)} %pad_clamp_fusion.3), kind=kCustom, calls=%fused_computation.clone | custom fusion | bytes 33554496 | tf_op jit(solution)/shard_map/jit(_take)/gather | solution.py:101
  728.1 10.5 %gather_fusion.10 = bf16[16,128,16,256]{3,1,2,0:T(8,128)(2,1)} fusion(bf16[8,128,16,256]{3,1,2,0:T(8,128)(2,1)} %copy.69, s32[1024]{0:T(1024)S(1)} %pad_clamp_fusion.1), kind=kCustom, calls=%fused_computation.4.clone | custom fusion | bytes 33554496 | tf_op jit(solution)/shard_map/jit(_take)/gather | solution.py:101
  738.6 22.6 %maximum_select_fusion = bf16[16,256,16,256]{3,1,2,0:T(8,128)(2,1)} fusion(bf16[16,128,16,256]{3,1,2,0:T(8,128)(2,1)} %gather_fusion.7, bf16[16,128,16,256]{3,1,2,0:T(8,128)(2,1)} %gather_fusion.6, pred[16]{0:T(512)(128)(4,1)S(1)} %get-tuple-element.39), kind=kLoop, calls=%fused_computation.14 | loop fusion | flops 83886080 | bytes 67108880 | tf_op jit(solution)/shard_map/jit(_take)/select_n | solution.py:101
  761.3 23.3 %fusion.17 = (bf16[16,128,16,256]{3,1,2,0:T(8,128)(2,1)}, bf16[16,128,16,256]{3,1,2,0:T(8,128)(2,1)}) fusion(bf16[16,256,16,256]{3,1,2,0:T(8,128)(2,1)} %maximum_select_fusion), kind=kLoop, calls=%fused_computation.101 | loop fusion | bytes 67108864 | tf_op jit(solution)/shard_map/jit(_take)/gather | solution.py:102
  784.6 10.3 %gather_fusion.8 = bf16[8,16,128,256]{3,2,1,0:T(8,128)(2,1)} fusion(bf16[16,128,16,256]{3,1,2,0:T(8,128)(2,1)} %get-tuple-element.26, s32[1024]{0:T(1024)} %pad_clamp_fusion.2), kind=kCustom, calls=%fused_computation.2.clone | custom fusion | bytes 16777248 | tf_op jit(solution)/shard_map/jit(_take)/gather | solution.py:102
  794.9 10.4 %gather_fusion.9 = bf16[8,16,128,256]{3,2,1,0:T(8,128)(2,1)} fusion(bf16[16,128,16,256]{3,1,2,0:T(8,128)(2,1)} %get-tuple-element.27, s32[1024]{0:T(1024)} %pad_clamp_fusion.2), kind=kCustom, calls=%fused_computation.3.clone | custom fusion | bytes 16777248 | tf_op jit(solution)/shard_map/jit(_take)/gather | solution.py:102
  805.4 22.6 %maximum_select_fusion.1 = bf16[16,256,16,256]{3,1,2,0:T(8,128)(2,1)} fusion(bf16[16,128,16,256]{3,1,2,0:T(8,128)(2,1)} %gather_fusion.11, bf16[16,128,16,256]{3,1,2,0:T(8,128)(2,1)} %gather_fusion.10, pred[16]{0:T(512)(128)(4,1)S(1)} %copy-done.9), kind=kLoop, calls=%fused_computation.15 | loop fusion | flops 83886080 | bytes 67108880 | tf_op jit(solution)/shard_map/jit(_take)/select_n | solution.py:101
  828.0 23.3 %fusion.16 = (bf16[16,128,16,256]{3,1,2,0:T(8,128)(2,1)}, bf16[16,128,16,256]{3,1,2,0:T(8,128)(2,1)}) fusion(bf16[16,256,16,256]{3,1,2,0:T(8,128)(2,1)} %maximum_select_fusion.1), kind=kLoop, calls=%fused_computation.100 | loop fusion | bytes 67108864 | tf_op jit(solution)/shard_map/jit(_take)/gather | solution.py:102
  851.4 10.3 %gather_fusion.12 = bf16[8,16,128,256]{3,2,1,0:T(8,128)(2,1)} fusion(bf16[16,128,16,256]{3,1,2,0:T(8,128)(2,1)} %get-tuple-element.24, s32[1024]{0:T(1024)} %pad_clamp_fusion), kind=kCustom, calls=%fused_computation.6.clone | custom fusion | bytes 16777248 | tf_op jit(solution)/shard_map/jit(_take)/gather | solution.py:102
  861.7 10.5 %gather_fusion.13 = bf16[8,16,128,256]{3,2,1,0:T(8,128)(2,1)} fusion(bf16[16,128,16,256]{3,1,2,0:T(8,128)(2,1)} %get-tuple-element.25, s32[1024]{0:T(1024)} %pad_clamp_fusion), kind=kCustom, calls=%fused_computation.7.clone | custom fusion | bytes 16777248 | tf_op jit(solution)/shard_map/jit(_take)/gather | solution.py:102
  872.3 22.2 %fusion = bf16[16,1,256,8,1,256]{5,2,0,3,4,1:T(8,128)(2,1)S(1)} fusion(f32[16,256,8,256]{3,1,0,2:T(8,128)} %copy.63, bf16[16,128,8,256]{3,1,0,2:T(8,128)(2,1)} %bitcast.96, bf16[16,128,8,256]{3,1,0,2:T(8,128)(2,1)} %bitcast.95, bf16[16,128,8,256]{3,1,0,2:T(8,128)(2,1)} %bitcast.98, bf16[16,128,8,256]{3,1,0,2:T(8,128)(2,1)} %bitcast.97, ...), kind=kLoop, calls=%fused_computation.18 | loop fusion | flops 142606336 | bytes 83886352 | tf_op jit(solution)/shard_map/reshape | solution.py:110
  894.5 11.1 %copy.66 = bf16[16,1,256,8,1,256]{5,3,4,2,1,0:T(8,128)(2,1)} copy(bf16[16,1,256,8,1,256]{5,2,0,3,4,1:T(8,128)(2,1)S(1)} %fusion) | data formatting | bytes 33554432 | tf_op jit(solution)/shard_map/reshape | solution.py:110
  (87 shorter events, 58.3 us)
Async XLA Ops:
  6.5 576.5 %copy-start = (bf16[256,256]{1,0:T(8,128)(2,1)S(1)}, bf16[256,256]{1,0:T(8,128)(2,1)}, u32[]{:S(2)}) copy-start(bf16[256,256]{1,0:T(8,128)(2,1)} %param.20) | copy-start | bytes 393220
  6.5 39.5 %all-gather.12.cloned.1.call-start = ((), (), s32[]{:S(2)}) async-start(), calls=%async_computation.5 | async-start | bytes 1179648 | tf_op jit(solution)/shard_map/all_gather | solution.py:42
  7.3 68.3 %all-gather.10.cloned.1.call-start = ((), (), s32[]{:S(2)}) async-start(), calls=%async_computation.4 | async-start | bytes 1179648 | tf_op jit(solution)/shard_map/all_gather | solution.py:54
  22.6 54.5 %copy-start.2 = (bf16[1,256,256]{2,1,0:T(8,128)(2,1)S(1)}, bf16[1,256,256]{2,1,0:T(8,128)(2,1)}, u32[]{:S(2)}) copy-start(bf16[1,256,256]{2,1,0:T(8,128)(2,1)} %param.16) | copy-start | bytes 393220
  340.8 8.7 copy-start.6
  340.8 11.6 %copy-start.3 = (f32[16,1,256]{2,1,0:T(1,128)S(1)}, f32[16,1,256]{2,1,0:T(1,128)}, u32[]{:S(2)}) copy-start(f32[16,1,256]{2,1,0:T(1,128)} %param.21) | copy-start | bytes 49156
  340.8 328.4 %all-to-all-start.1 = ((bf16[8,256,16,256]{3,1,0,2:T(8,128)(2,1)}), bf16[8,256,16,256]{3,1,0,2:T(8,128)(2,1)}, u32[]{:S(2)}, u32[]{:S(2)}) async-start(bf16[8,256,16,256]{3,1,0,2:T(8,128)(2,1)} %copy.60), calls=%async_computation.1 | async-start | bytes 33554432 | tf_op jit(solution)/shard_map/all_to_all | solution.py:98
  348.1 142.2 %all-gather.6.cloned.1.call-start = ((), (), s32[]{:S(2)}) async-start(), calls=%async_computation.2 | async-start | bytes 1179648 | tf_op jit(solution)/shard_map/all_gather | solution.py:43
  348.9 231.7 %all-gather.8.cloned.1.call-start = ((), (), s32[]{:S(2)}) async-start(), calls=%async_computation.3 | async-start | bytes 2228224 | tf_op jit(solution)/shard_map/all_gather | solution.py:74
  784.6 20.8 %copy-start.9 = (pred[16]{0:T(512)(128)(4,1)S(1)}, pred[16]{0:T(512)(128)(4,1)}, u32[]{:S(2)}) copy-start(pred[16]{0:T(512)(128)(4,1)} %get-tuple-element.38) | copy-start | bytes 52
  851.4 20.9 %copy-start.4 = (pred[16,8]{0,1:T(8,128)(4,1)S(1)}, pred[16,8]{0,1:T(8,128)(4,1)}, u32[]{:S(2)}) copy-start(pred[16,8]{0,1:T(8,128)(4,1)} %get-tuple-element.30) | copy-start | bytes 388
  851.4 20.9 %copy-start.5 = (pred[16,8]{0,1:T(8,128)(4,1)S(1)}, pred[16,8]{0,1:T(8,128)(4,1)}, u32[]{:S(2)}) copy-start(pred[16,8]{0,1:T(8,128)(4,1)} %get-tuple-element.31) | copy-start | bytes 388
  851.4 20.9 %copy-start.7 = (pred[8]{0:T(512)(128)(4,1)S(1)}, pred[8]{0:T(512)(128)(4,1)}, u32[]{:S(2)}) copy-start(pred[8]{0:T(512)(128)(4,1)} %get-tuple-element.36) | copy-start | bytes 28
  851.4 20.9 %copy-start.8 = (pred[8]{0:T(512)(128)(4,1)S(1)}, pred[8]{0:T(512)(128)(4,1)}, u32[]{:S(2)}) copy-start(pred[8]{0:T(512)(128)(4,1)} %get-tuple-element.37) | copy-start | bytes 28
  872.3 33.3 %copy-start.1 = (bf16[256,256]{1,0:T(8,128)(2,1)S(1)}, bf16[256,256]{1,0:T(8,128)(2,1)}, u32[]{:S(2)}) copy-start(bf16[256,256]{1,0:T(8,128)(2,1)} %param.20) | copy-start | bytes 393220
Sparse Core Ops, SparseCore 0:
  9.0 37.0 all-gather.11
  47.8 27.7 all-gather.9
  350.6 139.6 all-gather.5
  492.6 87.8 all-gather.7
where the time goes:
time: 918 us; the launch traced here: 912 us
  local copies, waits for them, and re-layouts  363 us (40%)
  waiting for transfers between devices  218 us (24%)
  blocking collectives  188 us (20%)
  other arithmetic  92.2 us (10%)
  matrix products  30.8 us (3%)
  between operations  13.6 us (1%)
    all_to_all x1, blocking collectives, shards(): lax.all_to_all(packed, 'row', split_axis=0, concat_axis=0, tiled=True)  188 us
    unnamed x31, local copies, waits for them, and re-layouts  113 us
    all_gather x1, waiting for transfers between devices, shards(): lax.all_gather(parent_row, 'row', axis=0, tiled=True)  93.5 us
    all_gather x1, waiting for transfers between devices, shards(): piece = lax.all_gather(parent_col, ('half', 'col'), axis=0, tiled=True)  88.7 us
    gather x6, local copies, waits for them, and re-layouts, shards(): jnp.take(picked, sibling * grid_size + col_source[sibling], axis=2)  88.3 us
    gather x5, local copies, waits for them, and re-layouts, shards(): picked = jnp.take(arrived, row_source[sibling], axis=0)  54 us
    select_n x3, other arithmetic, shards(): picked = jnp.take(arrived, row_source[sibling], axis=0)  45.3 us
    reshape x1, local copies, waits for them, and re-layouts, shards(): parent_front.reshape(2 * grid_size, tile_width, grid_size, tile_width)  34.4 us
  transfers between devices with their start and end apart: 5, of which 4 were waited for; matrix products, arithmetic and copies ran while one was open for 19% of the time, Pallas kernels for 0%

commit v1 on v0

--- a/solution.py
+++ b/solution.py
@@ -2,6 +2,13 @@
 import jax.numpy as jnp
 from jax import lax
 from jax.sharding import PartitionSpec as P
+
+
+def link_the_rings(raw, dim_no=0):
+    response = lax.psum(1, ("half", "col"))
+    placed = jnp.stack(response * [raw], axis=0)
+    block_now = lax.all_to_all(placed, ("half", "col"), 0, 0)
+    return jnp.concatenate(block_now, axis=dim_no)
 
 
 def inverse_maps(child_map, parent_tiles):
@@ -71,7 +78,7 @@
     diag_term = (
         diag_values[:, :, None, None] * on_diagonal[:, None, :, None] * identity[None, :, None, :]
     ).reshape(parent_height, local_width)
-    piece = lax.all_gather(parent_col, ("half", "col"), axis=0, tiled=True)
+    piece = link_the_rings(parent_col)
     piece_rows = piece.shape[0]
     flattened = piece.reshape(piece_rows, parent_height)
     scaled_part = parent_scaled

time: 918 us -> 863 us (0.940)
  waiting for transfers between devices: 218 us -> 135 us
  local copies, waits for them, and re-layouts: 363 us -> 375 us
    all_gather x1 -> x0, waiting for transfers between devices: 88.7 us -> none  [shards(): piece = lax.all_gather(parent_col, ('half', 'col'), axis=0, tiled=True)]
    all_to_all x0 -> x1, waiting for transfers between devices: none -> 14.5 us  [link_the_rings(): block_now = lax.all_to_all(placed, ('half', 'col'), 0, 0)]
    unnamed x31 -> x35, local copies, waits for them, and re-layouts: 113 us -> 116 us
  transfers between devices with their start and end apart: 5 -> 5, of which waited for: 4 -> 4; matrix products, arithmetic and copies ran while one was open for 19% -> 23% of each run, Pallas kernels for 0% -> 0%
where the time goes in v1:
time: 863 us; the launch traced here: 854 us
  local copies, waits for them, and re-layouts  375 us (43%)
  blocking collectives  188 us (22%)
  waiting for transfers between devices  135 us (16%)
  other arithmetic  99.1 us (11%)
  matrix products  30.8 us (4%)
  between operations  13.6 us (2%)
  starting transfers between devices  12.9 us (1%)
    all_to_all x1, blocking collectives, shards(): lax.all_to_all(packed, 'row', split_axis=0, concat_axis=0, tiled=True)  188 us
    unnamed x35, local copies, waits for them, and re-layouts  116 us
    gather x6, local copies, waits for them, and re-layouts, shards(): jnp.take(picked, sibling * grid_size + col_source[sibling], axis=2)  88.3 us
    all_gather x1, waiting for transfers between devices, shards(): lax.all_gather(parent_row, 'row', axis=0, tiled=True)  85.6 us
    gather x5, local copies, waits for them, and re-layouts, shards(): picked = jnp.take(arrived, row_source[sibling], axis=0)  54 us
    select_n x3, other arithmetic, shards(): picked = jnp.take(arrived, row_source[sibling], axis=0)  45.3 us
    reshape x1, local copies, waits for them, and re-layouts, shards(): parent_front.reshape(2 * grid_size, tile_width, grid_size, tile_width)  34.6 us
    dot_general x2, matrix products, shards(): lax.dot_general(flattened, scaled_part, (((0,), (0,)), ((), ())), preferr...  30.8 us
  transfers between devices with their start and end apart: 5, of which 4 were waited for; matrix products, arithmetic and copies ran while one was open for 23% of the time, Pallas kernels for 0%

profile of v1, /device:TPU:1, one launch (start us, length us, event | category | flops | bytes accessed | tf_op | source)
XLA Modules:
  0.0 854.4 jit_solution(10321642685640710645)
XLA Ops:
  8.8 13.8 %copy.75 = f32[256,8,8,256]{3,1,2,0:T(8,128)} copy(bf16[256,8,8,256]{3,2,1,0:T(8,128)(2,1)} %bitcast.102) | data formatting | bytes 25165824
  22.6 18.1 %copy.67 = f32[2048,2048]{0,1:T(8,128)} copy(f32[2048,2048]{1,0:T(8,128)} %bitcast.95) | data formatting | bytes 33554432 | tf_op jit(solution)/shard_map/convert_element_type | solution.py:69
  47.6 28.0 %all-gather.7.cloned.1.call-done = bf16[1,256,8,1,256]{4,2,3,0,1:T(8,128)(2,1)} async-done(((bf16[1,32,8,1,256]{4,2,3,0,1:T(8,128)(2,1)}), bf16[1,256,8,1,256]{4,2,3,0,1:T(8,128)(2,1)}) %all-gather.7.cloned.1.call-update) | async-done | bytes 1048592 | tf_op jit(solution)/shard_map/all_gather | solution.py:61
  77.2 9.3 %fusion.1 = bf16[2048,2048]{0,1:T(8,128)(2,1)} fusion(f32[2048,2048]{0,1:T(8,128)} %copy.67, bf16[256,2048]{1,0:T(8,128)(2,1)S(1)} %bitcast.107, bf16[256,2048]{1,0:T(8,128)(2,1)S(1)} %bitcast.106, bf16[1,256,256]{2,1,0:T(8,128)(2,1)S(1)} %copy-done.3), kind=kOutput, calls=%fused_computation.22 | convolution fusion | flops 2424832000 | bytes 27394048 | tf_op jit(solution)/shard_map/dot_general | solution.py:65
  86.5 10.3 %copy.78 = bf16[256,8,8,256]{3,2,1,0:T(8,128)(2,1)} copy(bf16[256,8,8,256]{3,1,2,0:T(8,128)(2,1)} %bitcast.100) | data formatting | bytes 16777216
  96.8 12.6 %copy.58 = bf16[8,256,8,256]{3,1,2,0:T(8,128)(2,1)} copy(bf16[8,256,8,256]{1,0,3,2:T(8,128)(2,1)} %bitcast.101) | data formatting | bytes 16777216 | tf_op jit(solution)/shard_map/reshape | solution.py:71
  124.8 10.7 %gather_fusion.3 = bf16[16,8,256,256]{3,2,1,0:T(8,128)(2,1)} fusion(bf16[8,256,8,256]{3,1,2,0:T(8,128)(2,1)} %broadcast_select_fusion, s32[1024]{0:T(1024)S(1)} %pad_clamp_fusion.4), kind=kCustom, calls=%fused_computation.11 | custom fusion | bytes 33554496 | tf_op jit(solution)/shard_map/jit(_take)/gather | solution.py:102
  135.6 8.7 %select_bitcast_fusion = bf16[8,256,16,256]{3,1,0,2:T(8,128)(2,1)S(1)} fusion(bf16[16,8,256,256]{3,2,1,0:T(8,128)(2,1)} %gather_fusion.3, pred[16]{0:T(512)(128)(4,1)S(1)} %fusion.8, pred[16]{0:T(512)(128)(4,1)S(1)} %compare_and_fusion.5), kind=kLoop, calls=%fused_computation.23 | loop fusion | flops 16777216 | bytes 33554464 | tf_op jit(solution)/shard_map/jit(_where)/select_n | solution.py:103
  146.6 188.0 %all_to_all.15 = bf16[8,256,16,256]{3,1,2,0:T(8,128)(2,1)} all-to-all(bf16[8,256,16,256]{3,1,2,0:T(8,128)(2,1)S(1)} %copy.59), channel_id=1, replica_groups=mesh['half'=2,'row'=8,'col'=8] {'row'}, dimensions={0} | all-to-all | bytes 33554432 | tf_op jit(solution)/shard_map/all_to_all | solution.py:104
  343.3 14.0 %copy.60 = bf16[8,256,16,256]{3,1,0,2:T(8,128)(2,1)} copy(bf16[8,256,16,256]{3,1,2,0:T(8,128)(2,1)} %all_to_all.15) | data formatting | bytes 33554432 | tf_op jit(solution)/shard_map/all_to_all | solution.py:104
  357.3 14.5 %all-to-all-done = bf16[16,16,16,1,256]{4,2,1,3,0:T(8,128)(2,1)S(1)} async-done(((bf16[16,16,16,1,256]{4,2,1,3,0:T(8,128)(2,1)}), bf16[16,16,16,1,256]{4,2,1,3,0:T(8,128)(2,1)S(1)}, u32[]{:S(2)}, u32[]{:S(2)}) %all-to-all-start) | async-done | bytes 2097184 | tf_op jit(solution)/shard_map/all_to_all | solution.py:10
  380.9 11.4 %broadcast_multiply_fusion = f32[16,256,8,256]{1,0,3,2:T(8,128)} fusion(f32[256,256]{0,1:T(8,128)S(1)} %fusion.2, f32[16,256,8]{1,0,2:T(8,128)S(1)} %broadcast_multiply_fusion.1), kind=kLoop, calls=%fused_computation.24 | loop fusion | flops 8388608 | bytes 33947648 | tf_op jit(solution)/shard_map/mul | solution.py:79
  394.3 37.9 %copy.71 = f32[256,8,16,256]{3,1,2,0:T(8,128)} copy(f32[256,8,16,256]{3,2,1,0:T(8,128)} %bitcast.93) | data formatting | bytes 67108864
  435.5 85.6 %all-gather.5.cloned.1.call-done = bf16[256,8,1,256]{3,1,2,0:T(8,128)(2,1)} async-done(((bf16[32,8,1,256]{3,1,2,0:T(8,128)(2,1)}), bf16[256,8,1,256]{3,1,2,0:T(8,128)(2,1)}) %all-gather.5.cloned.1.call-update) | async-done | bytes 1048592 | tf_op jit(solution)/shard_map/all_gather | solution.py:50
  525.1 21.5 %bitcast_subtract_fusion = f32[4096,2048]{0,1:T(8,128)} fusion(f32[4096,2048]{0,1:T(8,128)} %bitcast.91, bf16[256,4096]{1,0:T(8,128)(2,1)S(1)} %bitcast.103, bf16[256,256]{1,0:T(8,128)(2,1)S(1)} %copy-done, bf16[256,2048]{1,0:T(8,128)(2,1)S(1)} %bitcast.105), kind=kOutput, calls=%fused_computation.16 | convolution fusion | flops 4572315648 | bytes 70385664 | tf_op jit(solution)/shard_map/dot_general | solution.py:85
  546.6 30.2 %copy.74 = f32[256,8,16,256]{3,2,1,0:T(8,128)} copy(f32[256,8,16,256]{3,1,2,0:T(8,128)} %bitcast.92) | data formatting | bytes 67108864
  576.7 34.6 %copy.63 = f32[16,256,8,256]{3,1,0,2:T(8,128)} copy(f32[16,256,8,256]{1,0,3,2:T(8,128)} %bitcast.94) | data formatting | bytes 67108864 | tf_op jit(solution)/shard_map/reshape | solution.py:110
  611.3 12.0 %fusion.18 = (bf16[8,128,16,256]{3,1,0,2:T(8,128)(2,1)}, bf16[8,128,16,256]{3,1,0,2:T(8,128)(2,1)}) fusion(bf16[8,256,16,256]{3,1,0,2:T(8,128)(2,1)} %all-to-all-done.2), kind=kLoop, calls=%fused_computation.102 | loop fusion | bytes 33554432 | tf_op jit(solution)/shard_map/jit(_take)/gather | solution.py:108
  638.7 10.5 %gather_fusion.11 = bf16[16,128,16,256]{3,1,2,0:T(8,128)(2,1)} fusion(bf16[8,128,16,256]{3,1,2,0:T(8,128)(2,1)} %copy.70, s32[1024]{0:T(1024)S(1)} %pad_clamp_fusion.1), kind=kCustom, calls=%fused_computation.5.clone | custom fusion | bytes 33554496 | tf_op jit(solution)/shard_map/jit(_take)/gather | solution.py:108
  649.2 10.6 %gather_fusion.7 = bf16[16,128,16,256]{3,1,2,0:T(8,128)(2,1)} fusion(bf16[8,128,16,256]{3,1,2,0:T(8,128)(2,1)} %copy.70, s32[1024]{0:T(1024)S(1)} %pad_clamp_fusion.3), kind=kCustom, calls=%fused_computation.1.clone | custom fusion | bytes 33554496 | tf_op jit(solution)/shard_map/jit(_take)/gather | solution.py:108
  659.8 10.4 %gather_fusion.6 = bf16[16,128,16,256]{3,1,2,0:T(8,128)(2,1)} fusion(bf16[8,128,16,256]{3,1,2,0:T(8,128)(2,1)} %copy.69, s32[1024]{0:T(1024)S(1)} %pad_clamp_fusion.3), kind=kCustom, calls=%fused_computation.clone | custom fusion | bytes 33554496 | tf_op jit(solution)/shard_map/jit(_take)/gather | solution.py:108
  670.2 10.5 %gather_fusion.10 = bf16[16,128,16,256]{3,1,2,0:T(8,128)(2,1)} fusion(bf16[8,128,16,256]{3,1,2,0:T(8,128)(2,1)} %copy.69, s32[1024]{0:T(1024)S(1)} %pad_clamp_fusion.1), kind=kCustom, calls=%fused_computation.4.clone | custom fusion | bytes 33554496 | tf_op jit(solution)/shard_map/jit(_take)/gather | solution.py:108
  680.7 22.7 %maximum_select_fusion = bf16[16,256,16,256]{3,1,2,0:T(8,128)(2,1)} fusion(bf16[16,128,16,256]{3,1,2,0:T(8,128)(2,1)} %gather_fusion.7, bf16[16,128,16,256]{3,1,2,0:T(8,128)(2,1)} %gather_fusion.6, pred[16]{0:T(512)(128)(4,1)S(1)} %get-tuple-element.39), kind=kLoop, calls=%fused_computation.14 | loop fusion | flops 83886080 | bytes 67108880 | tf_op jit(solution)/shard_map/jit(_take)/select_n | solution.py:108
  703.4 23.3 %fusion.17 = (bf16[16,128,16,256]{3,1,2,0:T(8,128)(2,1)}, bf16[16,128,16,256]{3,1,2,0:T(8,128)(2,1)}) fusion(bf16[16,256,16,256]{3,1,2,0:T(8,128)(2,1)} %maximum_select_fusion), kind=kLoop, calls=%fused_computation.101 | loop fusion | bytes 67108864 | tf_op jit(solution)/shard_map/jit(_take)/gather | solution.py:109
  726.7 10.3 %gather_fusion.8 = bf16[8,16,128,256]{3,2,1,0:T(8,128)(2,1)} fusion(bf16[16,128,16,256]{3,1,2,0:T(8,128)(2,1)} %get-tuple-element.26, s32[1024]{0:T(1024)} %pad_clamp_fusion.2), kind=kCustom, calls=%fused_computation.2.clone | custom fusion | bytes 16777248 | tf_op jit(solution)/shard_map/jit(_take)/gather | solution.py:109
  737.0 10.4 %gather_fusion.9 = bf16[8,16,128,256]{3,2,1,0:T(8,128)(2,1)} fusion(bf16[16,128,16,256]{3,1,2,0:T(8,128)(2,1)} %get-tuple-element.27, s32[1024]{0:T(1024)} %pad_clamp_fusion.2), kind=kCustom, calls=%fused_computation.3.clone | custom fusion | bytes 16777248 | tf_op jit(solution)/shard_map/jit(_take)/gather | solution.py:109
  747.5 22.7 %maximum_select_fusion.1 = bf16[16,256,16,256]{3,1,2,0:T(8,128)(2,1)} fusion(bf16[16,128,16,256]{3,1,2,0:T(8,128)(2,1)} %gather_fusion.11, bf16[16,128,16,256]{3,1,2,0:T(8,128)(2,1)} %gather_fusion.10, pred[16]{0:T(512)(128)(4,1)S(1)} %copy-done.11), kind=kLoop, calls=%fused_computation.15 | loop fusion | flops 83886080 | bytes 67108880 | tf_op jit(solution)/shard_map/jit(_take)/select_n | solution.py:108
  770.1 23.3 %fusion.16 = (bf16[16,128,16,256]{3,1,2,0:T(8,128)(2,1)}, bf16[16,128,16,256]{3,1,2,0:T(8,128)(2,1)}) fusion(bf16[16,256,16,256]{3,1,2,0:T(8,128)(2,1)} %maximum_select_fusion.1), kind=kLoop, calls=%fused_computation.100 | loop fusion | bytes 67108864 | tf_op jit(solution)/shard_map/jit(_take)/gather | solution.py:109
  793.5 10.3 %gather_fusion.12 = bf16[8,16,128,256]{3,2,1,0:T(8,128)(2,1)} fusion(bf16[16,128,16,256]{3,1,2,0:T(8,128)(2,1)} %get-tuple-element.24, s32[1024]{0:T(1024)} %pad_clamp_fusion), kind=kCustom, calls=%fused_computation.6.clone | custom fusion | bytes 16777248 | tf_op jit(solution)/shard_map/jit(_take)/gather | solution.py:109
  803.8 10.5 %gather_fusion.13 = bf16[8,16,128,256]{3,2,1,0:T(8,128)(2,1)} fusion(bf16[16,128,16,256]{3,1,2,0:T(8,128)(2,1)} %get-tuple-element.25, s32[1024]{0:T(1024)} %pad_clamp_fusion), kind=kCustom, calls=%fused_computation.7.clone | custom fusion | bytes 16777248 | tf_op jit(solution)/shard_map/jit(_take)/gather | solution.py:109
  814.4 22.2 %fusion = bf16[16,1,256,8,1,256]{5,2,0,3,4,1:T(8,128)(2,1)S(1)} fusion(f32[16,256,8,256]{3,1,0,2:T(8,128)} %copy.63, bf16[16,128,8,256]{3,1,0,2:T(8,128)(2,1)} %bitcast.97, bf16[16,128,8,256]{3,1,0,2:T(8,128)(2,1)} %bitcast.96, bf16[16,128,8,256]{3,1,0,2:T(8,128)(2,1)} %bitcast.99, bf16[16,128,8,256]{3,1,0,2:T(8,128)(2,1)} %bitcast.98, ...), kind=kLoop, calls=%fused_computation.18 | loop fusion | flops 142606336 | bytes 83886352 | tf_op jit(solution)/shard_map/reshape | solution.py:117
  836.6 11.1 %copy.66 = bf16[16,1,256,8,1,256]{5,3,4,2,1,0:T(8,128)(2,1)} copy(bf16[16,1,256,8,1,256]{5,2,0,3,4,1:T(8,128)(2,1)S(1)} %fusion) | data formatting | bytes 33554432 | tf_op jit(solution)/shard_map/reshape | solution.py:117
  (91 shorter events, 70.9 us)
Async XLA Ops:
  6.5 518.5 %copy-start = (bf16[256,256]{1,0:T(8,128)(2,1)S(1)}, bf16[256,256]{1,0:T(8,128)(2,1)}, u32[]{:S(2)}) copy-start(bf16[256,256]{1,0:T(8,128)(2,1)} %param.20) | copy-start | bytes 393220
  6.5 39.5 %all-gather.9.cloned.1.call-start = ((), (), s32[]{:S(2)}) async-start(), calls=%async_computation.5 | async-start | bytes 1179648 | tf_op jit(solution)/shard_map/all_gather | solution.py:49
  7.3 68.4 %all-gather.7.cloned.1.call-start = ((), (), s32[]{:S(2)}) async-start(), calls=%async_computation.4 | async-start | bytes 1179648 | tf_op jit(solution)/shard_map/all_gather | solution.py:61
  22.6 54.6 %copy-start.3 = (bf16[1,256,256]{2,1,0:T(8,128)(2,1)S(1)}, bf16[1,256,256]{2,1,0:T(8,128)(2,1)}, u32[]{:S(2)}) copy-start(bf16[1,256,256]{2,1,0:T(8,128)(2,1)} %param.16) | copy-start | bytes 393220
  146.5 188.0 %copy-start.4 = (bf16[16,16,1,256]{3,1,2,0:T(8,128)(2,1)S(1)}, bf16[16,16,1,256]{3,1,2,0:T(8,128)(2,1)}, u32[]{:S(2)}) copy-start(bf16[16,16,1,256]{3,1,2,0:T(8,128)(2,1)} %param.19) | copy-start | bytes 393220
  336.1 35.7 %all-to-all-start = ((bf16[16,16,16,1,256]{4,2,1,3,0:T(8,128)(2,1)}), bf16[16,16,16,1,256]{4,2,1,3,0:T(8,128)(2,1)S(1)}, u32[]{:S(2)}, u32[]{:S(2)}) async-start(bf16[16,16,16,1,256]{4,2,1,3,0:T(8,128)(2,1)} %stack.2), calls=%async_computation | async-start | bytes 4194304 | tf_op jit(solution)/shard_map/all_to_all | solution.py:10
  357.3 22.2 %copy-start.5 = (f32[16,1,256]{2,1,0:T(1,128)S(1)}, f32[16,1,256]{2,1,0:T(1,128)}, u32[]{:S(2)}) copy-start(f32[16,1,256]{2,1,0:T(1,128)} %param.21) | copy-start | bytes 49156
  357.3 22.3 %copy-start.8 = (s32[2,64]{1,0:T(2,128)S(1)}, s32[2,64]{1,0:T(2,128)}, u32[]{:S(2)}) copy-start(s32[2,64]{1,0:T(2,128)} %param.17) | copy-start | bytes 1540
  371.8 1.3 copy-start.2
  373.1 238.2 %all-to-all-start.2 = ((bf16[8,256,16,256]{3,1,0,2:T(8,128)(2,1)}), bf16[8,256,16,256]{3,1,0,2:T(8,128)(2,1)}, u32[]{:S(2)}, u32[]{:S(2)}) async-start(bf16[8,256,16,256]{3,1,0,2:T(8,128)(2,1)} %copy.60), calls=%async_computation.2 | async-start | bytes 33554432 | tf_op jit(solution)/shard_map/all_to_all | solution.py:105
  378.8 142.2 %all-gather.5.cloned.1.call-start = ((), (), s32[]{:S(2)}) async-start(), calls=%async_computation.3 | async-start | bytes 1179648 | tf_op jit(solution)/shard_map/all_gather | solution.py:50
  726.7 20.8 %copy-start.11 = (pred[16]{0:T(512)(128)(4,1)S(1)}, pred[16]{0:T(512)(128)(4,1)}, u32[]{:S(2)}) copy-start(pred[16]{0:T(512)(128)(4,1)} %get-tuple-element.38) | copy-start | bytes 52
  793.5 20.9 %copy-start.6 = (pred[16,8]{0,1:T(8,128)(4,1)S(1)}, pred[16,8]{0,1:T(8,128)(4,1)}, u32[]{:S(2)}) copy-start(pred[16,8]{0,1:T(8,128)(4,1)} %get-tuple-element.30) | copy-start | bytes 388
  793.5 20.9 %copy-start.7 = (pred[16,8]{0,1:T(8,128)(4,1)S(1)}, pred[16,8]{0,1:T(8,128)(4,1)}, u32[]{:S(2)}) copy-start(pred[16,8]{0,1:T(8,128)(4,1)} %get-tuple-element.31) | copy-start | bytes 388
  793.5 20.9 %copy-start.9 = (pred[8]{0:T(512)(128)(4,1)S(1)}, pred[8]{0:T(512)(128)(4,1)}, u32[]{:S(2)}) copy-start(pred[8]{0:T(512)(128)(4,1)} %get-tuple-element.36) | copy-start | bytes 28
  793.5 20.9 %copy-start.10 = (pred[8]{0:T(512)(128)(4,1)S(1)}, pred[8]{0:T(512)(128)(4,1)}, u32[]{:S(2)}) copy-start(pred[8]{0:T(512)(128)(4,1)} %get-tuple-element.37) | copy-start | bytes 28
  814.4 33.3 %copy-start.1 = (bf16[256,256]{1,0:T(8,128)(2,1)S(1)}, bf16[256,256]{1,0:T(8,128)(2,1)}, u32[]{:S(2)}) copy-start(bf16[256,256]{1,0:T(8,128)(2,1)} %param.20) | copy-start | bytes 393220
Sparse Core Ops, SparseCore 0:
  9.0 37.0 all-gather.8
  47.8 27.8 all-gather.6
  381.2 139.7 all-gather.4
